TPU v7x, 32 devices: a whole 2x2x4 slice. The times are simulated.
32 devices in a mesh: rep: 2 (over y), cell: 4 (over z), sub: 4 (over x, core).
Axes of the slice: x: 2, y: 2, z: 4, core: 2. Of those that a mesh axis runs over, the one named last changes fastest.
Arguments:
- descriptors: bfloat16 [8, 4, 128, 128], P(('rep', 'cell'), 'sub'), parts along dimension 0, may hold values from -6 to 6
- positions: float32 [3, 8, 4, 128], P(None, ('rep', 'cell'), 'sub'), parts along dimension 1, may hold values from 0 to 4, as said below
- species: int32 [8, 4, 128], P(('rep', 'cell'), 'sub'), parts along dimension 0, may hold values from 0 to 3
- counts: int32 [8, 4], P(('rep', 'cell'), 'sub'), parts along dimension 0, may hold values from 80 to 128, as said below
- w_in: bfloat16 [8, 128, 256], replicated, may hold values from -0.5 to 0.5
- b_in: float32 [8, 256], replicated, may hold values from -3 to 3
- w_hid: bfloat16 [8, 256, 256], replicated, may hold values from -0.375 to 0.375
- b_hid: float32 [8, 256], replicated, may hold values from -3 to 3
- w_out: bfloat16 [8, 2, 256], replicated, may hold values from -0.375 to 0.375
Outputs:
- charges: float32 [8, 8, 4, 128], P(None, ('rep', 'cell'), 'sub'), parts along dimension 1
There are 2 independent parts, one for each index of `rep`. A program takes and returns all parts, laid end to end along the dimension named above; an argument that names none is the same for every part. Nothing has to cross between parts.
Inputs may be any that keep to these rules, and one draw needn't show every extreme that they name: `positions`: the first two coordinates of a slot lie between its cell's indices and one more, the height between 0 and 1. `counts`: a cell's slots from its count up are empty.
All inputs are finite; a program needn't handle non-finite values.
Results may differ from a plain program's by a relative error of at most 0.0003.
The roundings to bfloat16 on the way count: a program that leaves them out, or rounds other values in their place, can miss the bound.
Values sent between devices are 32-bit elements; how exact they have to be, the bound alone decides.
No kernel may reach another device: no remote copies, remote signals or barrier semaphores. Data moves between devices by JAX's collectives and lax.ppermute only.
A program may use at most 64 MiB of HBM per device.

v0:
```python
import jax
import jax.numpy as jnp
from jax import lax
from jax.sharding import PartitionSpec as P

ITERS = 2


def extended_2(shard, sides, width):
    for axis, dim in sides:
        size, length = (lax.axis_size(axis), shard.shape[dim])
        up = [(i, (i + 1) % size) for i in range(size - 1)]
        down = [(j, i) for i, j in up]
        last = lax.slice_in_dim(shard, length - width, length, axis=dim)
        leading = lax.slice_in_dim(shard, 0, width, axis=dim)
        before = lax.ppermute(last, axis, up)
        after = lax.ppermute(leading, axis, down)
        shard = jnp.concatenate([before, shard, after], axis=dim)
    return shard


def lookup(species, entries):
    choices_table = jnp.array(entries, jnp.float32)
    kinds = jnp.arange(4, dtype=jnp.int32)
    return jnp.sum((species[..., None] == kinds).astype(jnp.float32) * choices_table, axis=-1)


def coupling(own_atoms, far_atoms, self_cell):
    delta_a = own_atoms[0][..., :, None] - far_atoms[0][..., None, :]
    delta_b = own_atoms[1][..., :, None] - far_atoms[1][..., None, :]
    delta_c = own_atoms[2][..., :, None] - far_atoms[2][..., None, :]
    distance_sq = delta_a * delta_a + delta_b * delta_b + delta_c * delta_c
    radius = jnp.sqrt(distance_sq + 1e-06)
    pair_width = jnp.sqrt(own_atoms[3][..., :, None] ** 2 + far_atoms[3][..., None, :] ** 2)
    smooth_cut = (1.0 - jnp.minimum(distance_sq, 1.0)) ** 3
    kernel = 0.005 * smooth_cut * jax.scipy.special.erf(radius / pair_width) / radius
    kernel = kernel * own_atoms[4][..., :, None] * far_atoms[4][..., None, :]
    if self_cell:
        kernel = kernel * (1.0 - jnp.eye(kernel.shape[-1], dtype=jnp.float32))
    return kernel


def committee(flat_rows, w_in, b_in, w_hid, b_hid, w_out):

    def member_fn(weights):
        first_w, first_b, second_w, second_b, last_w = weights
        first = jnp.tanh(
            jnp.dot(flat_rows, first_w, preferred_element_type=jnp.float32) + first_b
        ).astype(jnp.bfloat16)
        second = jnp.tanh(
            jnp.dot(first, second_w, preferred_element_type=jnp.float32) + second_b
        ).astype(jnp.bfloat16)
        return jnp.dot(second, last_w.T, preferred_element_type=jnp.float32).T

    return lax.map(member_fn, (w_in, b_in, w_hid, b_hid, w_out))


def expand(values):
    return values[:, None, None, None]


def extend(vectors):
    return extended_2(vectors, (("cell", 1), ("sub", 2)), 1)


def two_products(residual, image_vec):
    return lax.psum(
        (
            jnp.sum(residual * residual, axis=(1, 2, 3)),
            jnp.sum(residual * image_vec, axis=(1, 2, 3)),
        ),
        ("cell", "sub"),
    )


def body(descriptors, positions, species, counts, w_in, b_in, w_hid, b_hid, w_out):
    rows_a, rows_b, slot_count, features = descriptors.shape
    members = w_in.shape[0]
    slot_iota = lax.broadcasted_iota(jnp.int32, (rows_a, rows_b, slot_count), 2)
    occupancy = (slot_iota < counts[:, :, None]).astype(jnp.float32)
    widths = lookup(species, (0.3, 0.4, 0.5, 0.35))
    shifts = lookup(species, (-0.8, 0.4, 1.2, -0.3))
    atom_data = jnp.stack([positions[0], positions[1], positions[2], widths, occupancy])
    extended = extended_2(atom_data, (("cell", 1), ("sub", 2)), 1)
    outputs = committee(descriptors.reshape(-1, features), w_in, b_in, w_hid, b_hid, w_out)
    electro = outputs[:, 0].reshape(members, rows_a, rows_b, slot_count) + shifts
    hardness = 2.5 + jax.nn.softplus(outputs[:, 1]).reshape(members, rows_a, rows_b, slot_count)
    right_side = jnp.concatenate([-electro * occupancy, jnp.broadcast_to(occupancy, electro.shape)])
    diagonal = jnp.concatenate([hardness, hardness])
    offsets = [(row_step, col_step) for row_step in (-1, 0, 1) for col_step in (-1, 0, 1)]

    def neighbours(grown, row_step, col_step):
        return grown[:, 1 + row_step : 1 + row_step + rows_a, 1 + col_step : 1 + col_step + rows_b]

    def block_for(row_step, col_step):
        return coupling(
            atom_data, neighbours(extended, row_step, col_step), row_step == 0 and col_step == 0
        )

    def operate(vectors):
        grown = extend(vectors)
        summed = diagonal * vectors
        for offset_number in range(9):
            row_step, col_step = offsets[offset_number]
            tile_block = block_for(row_step, col_step)
            summed = summed + jnp.einsum(
                "abij,rabj->rabi",
                tile_block,
                neighbours(grown, row_step, col_step),
                precision=lax.Precision.HIGHEST,
            )
        return summed

    solution = jnp.zeros_like(right_side)
    residual = right_side
    image_vec = operate(residual)
    norm_now, product = two_products(residual, image_vec)
    step_size = norm_now / product
    direction = residual
    along = image_vec
    for iteration in range(ITERS):
        solution = solution + expand(step_size) * direction
        residual = residual - expand(step_size) * along
        if iteration + 1 < ITERS:
            image_vec = operate(residual)
            norm_next, product = two_products(residual, image_vec)
            momentum = norm_next / norm_now
            step_size = norm_next / (product - momentum * norm_next / step_size)
            direction = residual + expand(momentum) * direction
            along = image_vec + expand(momentum) * along
            norm_now = norm_next
    source_part = solution[:members]
    unit_part = solution[members:]
    source_total, unit_total = lax.psum(
        (jnp.sum(source_part, axis=(1, 2, 3)), jnp.sum(unit_part, axis=(1, 2, 3))), ("cell", "sub")
    )
    multiplier = source_total / unit_total
    return source_part - expand(multiplier) * unit_part


def solution(mesh):
    placed = (
        P(("rep", "cell"), "sub", None, None),
        P(None, ("rep", "cell"), "sub", None),
        P(("rep", "cell"), "sub", None),
        P(("rep", "cell"), "sub"),
        P(),
        P(),
        P(),
        P(),
        P(),
    )
    return jax.shard_map(
        body,
        mesh=mesh,
        in_specs=placed,
        out_specs=P(None, ("rep", "cell"), "sub", None),
        check_vma=False,
    )
```

profile of v0, /device:TPU:0, one launch (start us, length us, event | category | flops | bytes accessed | tf_op | source)
XLA Modules:
  0.0 162.4 jit_solution(817328596570709719)
XLA Ops:
  0.7 24.5 %while.10 = (s32[]{:T(128)}, f32[8,2,128]{2,0,1:T(8,128)S(1)}, bf16[8,2,256]{2,1,0:T(2,128)(2,1)}, bf16[8,128,256]{2,1,0:T(8,128)(2,1)}, bf16[128,128]{1,0:T(8,1...) while((s32[]{:T(128)}, f32[8,2,128]{2,0,1:T(8,128)S(1)}, ...), condition=%wide.region_1.0_spmd, body=%wide.region_0.0_spmd.sunk | while | flops 25427968 | bytes 372333 | solution.py:55
  0.7 0.7 constant_dynamic-slice_fusion.4
  1.4 1.0 fusion.170
  2.5 1.2 fusion.171
  3.7 0.7 constant_dynamic-slice_fusion.4
  4.5 1.0 fusion.170
  5.5 1.2 fusion.171
  6.8 0.7 constant_dynamic-slice_fusion.4
  7.5 1.0 fusion.170
  8.6 1.2 fusion.171
  9.8 0.7 constant_dynamic-slice_fusion.4
  10.6 1.0 fusion.170
  11.6 1.2 fusion.171
  12.9 0.7 constant_dynamic-slice_fusion.4
  13.6 1.0 fusion.170
  14.7 1.2 fusion.171
  16.0 0.7 constant_dynamic-slice_fusion.4
  16.7 1.0 fusion.170
  17.7 1.2 fusion.171
  19.0 0.7 constant_dynamic-slice_fusion.4
  19.7 1.0 fusion.170
  20.8 1.2 fusion.171
  22.1 0.7 constant_dynamic-slice_fusion.4
  22.8 1.0 fusion.170
  23.8 1.2 fusion.171
  25.2 0.6 copy-done.1
  26.1 4.9 %collective-permute-start = (f32[16,1,1,128]{3,0,2,1:T(8,128)S(1)}, f32[16,1,1,128]{3,0,2,1:T(8,128)S(1)}, u32[]{:S(2)}, u32[]{:S(2)}) collective-permute-start(f32[16,1,1,128]{3,0,2,1:T(8,128)S(1)} %get-tuple-element.113), channel_id=1, source_target_pairs={{0,4},{4,8},{8,12},{1,5},{5,9},{9,13},{2,6},{6,10},{10,14},{3,7},{... | collective-permute-start | bytes 24584 | tf_op jit(solution)/shard_map/ppermute | solution.py:16
  31.0 1.3 collective-permute-start.1
  32.3 0.7 copy-done
  33.0 4.5 %collective-permute-start.3 = (f32[5,1,1,128]{3,2,1,0:T(1,128)S(1)}, f32[5,1,1,128]{3,2,1,0:T(1,128)S(1)}, u32[]{:S(2)}, u32[]{:S(2)}) collective-permute-start(f32[5,1,1,128]{3,2,1,0:T(1,128)S(1)} %pad_maximum_fusion.7), channel_id=1, source_target_pairs={{0,4},{4,8},{8,12},{1,5},{5,9},{9,13},{2,6},{6,10},{10,14},{3,7},{... | collective-permute-start | bytes 7688 | tf_op jit(solution)/shard_map/ppermute | solution.py:16
  37.5 1.3 collective-permute-start.4
  39.2 3.8 %collective-permute-done.4 = f32[5,1,1,128]{3,2,1,0:T(1,128)S(1)} collective-permute-done((f32[5,1,1,128]{3,2,1,0:T(1,128)S(1)}, f32[5,1,1,128]{3,2,1,0:T(1,128)S(1)}, u32[]{:S(2)}, u32[]{:S(2)}) %collective-permute-start.4) | collective-permute-done | bytes 2592 | tf_op jit(solution)/shard_map/ppermute | solution.py:17
  43.0 1.3 collective-permute-start.7
  44.3 3.0 %collective-permute-start.5 = (f32[5,3,1,128]{3,2,1,0:T(1,128)S(1)}, f32[5,3,1,128]{3,2,1,0:T(1,128)S(1)}, u32[]{:S(2)}, u32[]{:S(2)}) collective-permute-start(f32[5,3,1,128]{3,2,1,0:T(1,128)S(1)} %pad_maximum_fusion.6), channel_id=1, source_target_pairs={{0,1},{1,2},{2,3},{4,5},{5,6},{6,7},{8,9},{9,10},{10,11},{12,13},{... | collective-permute-start | bytes 23048 | tf_op jit(solution)/shard_map/ppermute | solution.py:16
  47.4 1.3 collective-permute-start.6
  48.7 3.6 %collective-permute-start.2 = (f32[16,3,1,128]{3,0,2,1:T(8,128)S(1)}, f32[16,3,1,128]{3,0,2,1:T(8,128)S(1)}, u32[]{:S(2)}, u32[]{:S(2)}) collective-permute-start(f32[16,3,1,128]{3,0,2,1:T(8,128)S(1)} %pad_maximum_fusion), channel_id=1, source_target_pairs={{0,1},{1,2},{2,3},{4,5},{5,6},{6,7},{8,9},{9,10},{10,11},{12,13},{... | collective-permute-start | bytes 73736 | tf_op jit(solution)/shard_map/ppermute | solution.py:16
  55.0 0.5 fusion.72
  55.5 32.3 %all-reduce.2 = (f32[16]{0:T(128)S(1)}, f32[16]{0:T(128)S(1)}) all-reduce(f32[16]{0:T(128)S(1)} %get-tuple-element.112, f32[16]{0:T(128)S(1)} %get-tuple-element.127), channel_id=1, replica_groups=mesh['rep'=2,'cell'=4,'sub'=4] {'cell','sub'}, use_global_device_ids=true, to_apply=%region_4.5 | all-reduce | flops 32 | bytes 256 | tf_op jit(solution)/shard_map/psum | solution.py:67
  87.9 1.3 collective-permute-start.8
  89.2 1.3 collective-permute-start.9
  90.9 3.9 %collective-permute-done.9 = f32[16,1,1,128]{3,0,2,1:T(8,128)S(1)} collective-permute-done((f32[16,1,1,128]{3,0,2,1:T(8,128)S(1)}, f32[16,1,1,128]{3,0,2,1:T(8,128)S(1)}, u32[]{:S(2)}, u32[]{:S(2)}) %collective-permute-start.9) | collective-permute-done | bytes 8224 | tf_op jit(solution)/shard_map/ppermute | solution.py:17
  94.8 1.3 collective-permute-start.11
  96.1 3.0 %collective-permute-start.10 = (f32[16,3,1,128]{3,0,2,1:T(8,128)S(1)}, f32[16,3,1,128]{3,0,2,1:T(8,128)S(1)}, u32[]{:S(2)}, u32[]{:S(2)}) collective-permute-start(f32[16,3,1,128]{3,0,2,1:T(8,128)S(1)} %pad_maximum_fusion.1), channel_id=1, source_target_pairs={{0,1},{1,2},{2,3},{4,5},{5,6},{6,7},{8,9},{9,10},{10,11},{12,13},{... | collective-permute-start | bytes 73736 | tf_op jit(solution)/shard_map/ppermute | solution.py:16
  101.3 0.4 fusion.24
  101.7 0.5 fusion.32
  102.2 29.8 %all-reduce.1 = (f32[16]{0:T(128)S(1)}, f32[16]{0:T(128)S(1)}) all-reduce(f32[16]{0:T(128)S(1)} %get-tuple-element.76, f32[16]{0:T(128)S(1)} %fusion.32), channel_id=1, replica_groups=mesh['rep'=2,'cell'=4,'sub'=4] {'cell','sub'}, use_global_device_ids=true, to_apply=%region_9.10 | all-reduce | flops 32 | bytes 256 | tf_op jit(solution)/shard_map/psum | solution.py:67
  132.3 29.5 %all-reduce = (f32[8]{0:T(128)S(1)}, f32[8]{0:T(128)S(1)}) all-reduce(f32[8]{0:T(128)S(1)} %get-tuple-element.49, f32[8]{0:T(128)S(1)} %get-tuple-element.48), channel_id=1, replica_groups=mesh['rep'=2,'cell'=4,'sub'=4] {'cell','sub'}, use_global_device_ids=true, to_apply=%region_13.14 | all-reduce | flops 16 | bytes 128 | tf_op jit(solution)/shard_map/psum | solution.py:134
  161.8 0.7 multiply_subtract_fusion
  (64 shorter events, 6.3 us)
Async XLA Ops:
  25.1 0.7 copy-start.1
  25.1 0.7 copy-start.2
  25.1 0.7 copy-start.3
  26.1 21.3 %collective-permute-start = (f32[16,1,1,128]{3,0,2,1:T(8,128)S(1)}, f32[16,1,1,128]{3,0,2,1:T(8,128)S(1)}, u32[]{:S(2)}, u32[]{:S(2)}) collective-permute-start(f32[16,1,1,128]{3,0,2,1:T(8,128)S(1)} %get-tuple-element.113), channel_id=1, source_target_pairs={{0,4},{4,8},{8,12},{1,5},{5,9},{9,13},{2,6},{6,10},{10,14},{3,7},{... | collective-permute-start | bytes 24584 | tf_op jit(solution)/shard_map/ppermute | solution.py:16
  31.0 16.4 %collective-permute-start.1 = (f32[16,1,1,128]{3,0,2,1:T(8,128)S(1)}, f32[16,1,1,128]{3,0,2,1:T(8,128)S(1)}, u32[]{:S(2)}, u32[]{:S(2)}) collective-permute-start(f32[16,1,1,128]{3,0,2,1:T(8,128)S(1)} %get-tuple-element.113), channel_id=1, source_target_pairs={{4,0},{8,4},{12,8},{5,1},{9,5},{13,9},{6,2},{10,6},{14,10},{7,3},{... | collective-permute-start | bytes 24584 | tf_op jit(solution)/shard_map/ppermute | solution.py:17
  32.3 0.7 copy-start
  33.0 6.2 %collective-permute-start.3 = (f32[5,1,1,128]{3,2,1,0:T(1,128)S(1)}, f32[5,1,1,128]{3,2,1,0:T(1,128)S(1)}, u32[]{:S(2)}, u32[]{:S(2)}) collective-permute-start(f32[5,1,1,128]{3,2,1,0:T(1,128)S(1)} %pad_maximum_fusion.7), channel_id=1, source_target_pairs={{0,4},{4,8},{8,12},{1,5},{5,9},{9,13},{2,6},{6,10},{10,14},{3,7},{... | collective-permute-start | bytes 7688 | tf_op jit(solution)/shard_map/ppermute | solution.py:16
  37.5 5.5 %collective-permute-start.4 = (f32[5,1,1,128]{3,2,1,0:T(1,128)S(1)}, f32[5,1,1,128]{3,2,1,0:T(1,128)S(1)}, u32[]{:S(2)}, u32[]{:S(2)}) collective-permute-start(f32[5,1,1,128]{3,2,1,0:T(1,128)S(1)} %pad_maximum_fusion.7), channel_id=1, source_target_pairs={{4,0},{8,4},{12,8},{5,1},{9,5},{13,9},{6,2},{10,6},{14,10},{7,3},{... | collective-permute-start | bytes 7688 | tf_op jit(solution)/shard_map/ppermute | solution.py:17
  43.0 10.0 %collective-permute-start.7 = (f32[5,3,1,128]{3,2,1,0:T(1,128)S(1)}, f32[5,3,1,128]{3,2,1,0:T(1,128)S(1)}, u32[]{:S(2)}, u32[]{:S(2)}) collective-permute-start(f32[5,3,1,128]{3,2,1,0:T(1,128)S(1)} %pad_maximum_fusion.6), channel_id=1, source_target_pairs={{1,0},{2,1},{3,2},{5,4},{6,5},{7,6},{9,8},{10,9},{11,10},{13,12},{... | collective-permute-start | bytes 23048 | tf_op jit(solution)/shard_map/ppermute | solution.py:17
  44.3 8.8 %collective-permute-start.5 = (f32[5,3,1,128]{3,2,1,0:T(1,128)S(1)}, f32[5,3,1,128]{3,2,1,0:T(1,128)S(1)}, u32[]{:S(2)}, u32[]{:S(2)}) collective-permute-start(f32[5,3,1,128]{3,2,1,0:T(1,128)S(1)} %pad_maximum_fusion.6), channel_id=1, source_target_pairs={{0,1},{1,2},{2,3},{4,5},{5,6},{6,7},{8,9},{9,10},{10,11},{12,13},{... | collective-permute-start | bytes 23048 | tf_op jit(solution)/shard_map/ppermute | solution.py:16
  47.4 6.5 %collective-permute-start.6 = (f32[16,3,1,128]{3,0,2,1:T(8,128)S(1)}, f32[16,3,1,128]{3,0,2,1:T(8,128)S(1)}, u32[]{:S(2)}, u32[]{:S(2)}) collective-permute-start(f32[16,3,1,128]{3,0,2,1:T(8,128)S(1)} %pad_maximum_fusion), channel_id=1, source_target_pairs={{1,0},{2,1},{3,2},{5,4},{6,5},{7,6},{9,8},{10,9},{11,10},{13,12},{... | collective-permute-start | bytes 73736 | tf_op jit(solution)/shard_map/ppermute | solution.py:17
  48.7 4.5 %collective-permute-start.2 = (f32[16,3,1,128]{3,0,2,1:T(8,128)S(1)}, f32[16,3,1,128]{3,0,2,1:T(8,128)S(1)}, u32[]{:S(2)}, u32[]{:S(2)}) collective-permute-start(f32[16,3,1,128]{3,0,2,1:T(8,128)S(1)} %pad_maximum_fusion), channel_id=1, source_target_pairs={{0,1},{1,2},{2,3},{4,5},{5,6},{6,7},{8,9},{9,10},{10,11},{12,13},{... | collective-permute-start | bytes 73736 | tf_op jit(solution)/shard_map/ppermute | solution.py:16
  87.9 2.9 %collective-permute-start.8 = (f32[16,1,1,128]{3,0,2,1:T(8,128)S(1)}, f32[16,1,1,128]{3,0,2,1:T(8,128)S(1)}, u32[]{:S(2)}, u32[]{:S(2)}) collective-permute-start(f32[16,1,1,128]{3,0,2,1:T(8,128)S(1)} %bitcast.216), channel_id=1, source_target_pairs={{0,4},{4,8},{8,12},{1,5},{5,9},{9,13},{2,6},{6,10},{10,14},{3,7},{... | collective-permute-start | bytes 24584 | tf_op jit(solution)/shard_map/ppermute | solution.py:16
  89.2 5.5 %collective-permute-start.9 = (f32[16,1,1,128]{3,0,2,1:T(8,128)S(1)}, f32[16,1,1,128]{3,0,2,1:T(8,128)S(1)}, u32[]{:S(2)}, u32[]{:S(2)}) collective-permute-start(f32[16,1,1,128]{3,0,2,1:T(8,128)S(1)} %bitcast.217), channel_id=1, source_target_pairs={{4,0},{8,4},{12,8},{5,1},{9,5},{13,9},{6,2},{10,6},{14,10},{7,3},{... | collective-permute-start | bytes 24584 | tf_op jit(solution)/shard_map/ppermute | solution.py:17
  94.8 5.8 %collective-permute-start.11 = (f32[16,3,1,128]{3,0,2,1:T(8,128)S(1)}, f32[16,3,1,128]{3,0,2,1:T(8,128)S(1)}, u32[]{:S(2)}, u32[]{:S(2)}) collective-permute-start(f32[16,3,1,128]{3,0,2,1:T(8,128)S(1)} %pad_maximum_fusion.1), channel_id=1, source_target_pairs={{1,0},{2,1},{3,2},{5,4},{6,5},{7,6},{9,8},{10,9},{11,10},{13,12},{... | collective-permute-start | bytes 73736 | tf_op jit(solution)/shard_map/ppermute | solution.py:17
  96.1 3.9 %collective-permute-start.10 = (f32[16,3,1,128]{3,0,2,1:T(8,128)S(1)}, f32[16,3,1,128]{3,0,2,1:T(8,128)S(1)}, u32[]{:S(2)}, u32[]{:S(2)}) collective-permute-start(f32[16,3,1,128]{3,0,2,1:T(8,128)S(1)} %pad_maximum_fusion.1), channel_id=1, source_target_pairs={{0,1},{1,2},{2,3},{4,5},{5,6},{6,7},{8,9},{9,10},{10,11},{12,13},{... | collective-permute-start | bytes 73736 | tf_op jit(solution)/shard_map/ppermute | solution.py:16
where the time goes:
time: 164 us; the launch traced here: 162 us
  blocking collectives  91.6 us (56%)
  starting transfers between devices  28.2 us (17%)
  matrix products  24.6 us (15%)
  waiting for transfers between devices  8.07 us (5%)
  local copies, waits for them, and re-layouts  7.33 us (4%)
    psum x2, blocking collectives, two_products(): lax.psum((jnp.sum(residual * residual, axis=(1, 2, 3)), jnp.sum(residual...  62.1 us
    psum x1, blocking collectives, body(): lax.psum((jnp.sum(source_part, axis=(1, 2, 3)), jnp.sum(unit_part, axis=(...  29.5 us
    ppermute x6, starting transfers between devices, extended_2(): before = lax.ppermute(last, axis, up)  20.5 us
    dot_general x8, matrix products, member_fn(): return jnp.dot(second, last_w.T, preferred_element_type=jnp.float32).T  9.96 us
    dot_general x8, matrix products, member_fn(): jnp.dot(flat_rows, first_w, preferred_element_type=jnp.float32) + first_b  8.33 us
    ppermute x6, waiting for transfers between devices, extended_2(): after = lax.ppermute(leading, axis, down)  7.78 us
    ppermute x6, starting transfers between devices, extended_2(): after = lax.ppermute(leading, axis, down)  7.74 us
    dot_general x18, matrix products, operate(): jnp.einsum('abij,rabj->rabi', tile_block, neighbours(grown, row_step, col...  6.36 us
  transfers between devices with their start and end apart: 12, of which 4 were waited for; matrix products, arithmetic and copies ran while one was open for 2% of the time, Pallas kernels for 0%

commit v1 on v0

--- a/solution.py
+++ b/solution.py
@@ -132,7 +132,8 @@
     source_part = solution[:members]
     unit_part = solution[members:]
     source_total, unit_total = lax.psum(
-        (jnp.sum(source_part, axis=(1, 2, 3)), jnp.sum(unit_part, axis=(1, 2, 3))), ("cell", "sub")
+        lax.psum((jnp.sum(source_part, axis=(1, 2, 3)), jnp.sum(unit_part, axis=(1, 2, 3))), "sub"),
+        "cell",
     )
     multiplier = source_total / unit_total
     return source_part - expand(multiplier) * unit_part

time: 164 us -> 149 us (0.909)
  blocking collectives: 91.6 us -> 76.2 us
    psum x1, blocking collectives: 29.5 us -> 5.76 us  [body(): lax.psum((jnp.sum(source_part, axis=(1, 2, 3)), jnp.sum(unit_part, axis=(...]
    psum x0 -> x1, blocking collectives: none -> 8.35 us  [body(): lax.psum(lax.psum((jnp.sum(source_part, axis=(1, 2, 3)), jnp.sum(unit_par...]
where the time goes in v1:
time: 149 us; the launch traced here: 147 us
  blocking collectives  76.2 us (51%)
  starting transfers between devices  28.2 us (19%)
  matrix products  24.6 us (17%)
  waiting for transfers between devices  8.07 us (5%)
  local copies, waits for them, and re-layouts  7.33 us (5%)
    psum x2, blocking collectives, two_products(): lax.psum((jnp.sum(residual * residual, axis=(1, 2, 3)), jnp.sum(residual...  62.1 us
    ppermute x6, starting transfers between devices, extended_2(): before = lax.ppermute(last, axis, up)  20.5 us
    dot_general x8, matrix products, member_fn(): return jnp.dot(second, last_w.T, preferred_element_type=jnp.float32).T  9.96 us
    psum x1, blocking collectives, body(): lax.psum(lax.psum((jnp.sum(source_part, axis=(1, 2, 3)), jnp.sum(unit_par...  8.35 us
    dot_general x8, matrix products, member_fn(): jnp.dot(flat_rows, first_w, preferred_element_type=jnp.float32) + first_b  8.33 us
    ppermute x6, waiting for transfers between devices, extended_2(): after = lax.ppermute(leading, axis, down)  7.78 us
    ppermute x6, starting transfers between devices, extended_2(): after = lax.ppermute(leading, axis, down)  7.74 us
    dot_general x18, matrix products, operate(): jnp.einsum('abij,rabj->rabi', tile_block, neighbours(grown, row_step, col...  6.36 us
  transfers between devices with their start and end apart: 12, of which 4 were waited for; matrix products, arithmetic and copies ran while one was open for 2% of the time, Pallas kernels for 0%

profile of v1, /device:TPU:0, one launch (start us, length us, event | category | flops | bytes accessed | tf_op | source)
XLA Modules:
  0.0 147.0 jit_solution(10411510981948046390)
XLA Ops:
  0.7 24.5 %while.10 = (s32[]{:T(128)}, f32[8,2,128]{2,0,1:T(8,128)S(1)}, bf16[8,2,256]{2,1,0:T(2,128)(2,1)}, bf16[8,128,256]{2,1,0:T(8,128)(2,1)}, bf16[128,128]{1,0:T(8,1...) while((s32[]{:T(128)}, f32[8,2,128]{2,0,1:T(8,128)S(1)}, ...), condition=%wide.region_1.0_spmd, body=%wide.region_0.0_spmd.sunk | while | flops 25427968 | bytes 372333 | solution.py:55
  0.7 0.7 constant_dynamic-slice_fusion.4
  1.4 1.0 fusion.170
  2.5 1.2 fusion.171
  3.7 0.7 constant_dynamic-slice_fusion.4
  4.5 1.0 fusion.170
  5.5 1.2 fusion.171
  6.8 0.7 constant_dynamic-slice_fusion.4
  7.5 1.0 fusion.170
  8.6 1.2 fusion.171
  9.8 0.7 constant_dynamic-slice_fusion.4
  10.6 1.0 fusion.170
  11.6 1.2 fusion.171
  12.9 0.7 constant_dynamic-slice_fusion.4
  13.6 1.0 fusion.170
  14.7 1.2 fusion.171
  16.0 0.7 constant_dynamic-slice_fusion.4
  16.7 1.0 fusion.170
  17.7 1.2 fusion.171
  19.0 0.7 constant_dynamic-slice_fusion.4
  19.7 1.0 fusion.170
  20.8 1.2 fusion.171
  22.1 0.7 constant_dynamic-slice_fusion.4
  22.8 1.0 fusion.170
  23.8 1.2 fusion.171
  25.2 0.6 copy-done.1
  26.1 4.9 %collective-permute-start = (f32[16,1,1,128]{3,0,2,1:T(8,128)S(1)}, f32[16,1,1,128]{3,0,2,1:T(8,128)S(1)}, u32[]{:S(2)}, u32[]{:S(2)}) collective-permute-start(f32[16,1,1,128]{3,0,2,1:T(8,128)S(1)} %get-tuple-element.115), channel_id=1, source_target_pairs={{0,4},{4,8},{8,12},{1,5},{5,9},{9,13},{2,6},{6,10},{10,14},{3,7},{... | collective-permute-start | bytes 24584 | tf_op jit(solution)/shard_map/ppermute | solution.py:16
  31.0 1.3 collective-permute-start.1
  32.3 0.7 copy-done
  33.0 4.5 %collective-permute-start.3 = (f32[5,1,1,128]{3,2,1,0:T(1,128)S(1)}, f32[5,1,1,128]{3,2,1,0:T(1,128)S(1)}, u32[]{:S(2)}, u32[]{:S(2)}) collective-permute-start(f32[5,1,1,128]{3,2,1,0:T(1,128)S(1)} %pad_maximum_fusion.7), channel_id=1, source_target_pairs={{0,4},{4,8},{8,12},{1,5},{5,9},{9,13},{2,6},{6,10},{10,14},{3,7},{... | collective-permute-start | bytes 7688 | tf_op jit(solution)/shard_map/ppermute | solution.py:16
  37.5 1.3 collective-permute-start.4
  39.2 3.8 %collective-permute-done.4 = f32[5,1,1,128]{3,2,1,0:T(1,128)S(1)} collective-permute-done((f32[5,1,1,128]{3,2,1,0:T(1,128)S(1)}, f32[5,1,1,128]{3,2,1,0:T(1,128)S(1)}, u32[]{:S(2)}, u32[]{:S(2)}) %collective-permute-start.4) | collective-permute-done | bytes 2592 | tf_op jit(solution)/shard_map/ppermute | solution.py:17
  43.0 1.3 collective-permute-start.7
  44.3 3.0 %collective-permute-start.5 = (f32[5,3,1,128]{3,2,1,0:T(1,128)S(1)}, f32[5,3,1,128]{3,2,1,0:T(1,128)S(1)}, u32[]{:S(2)}, u32[]{:S(2)}) collective-permute-start(f32[5,3,1,128]{3,2,1,0:T(1,128)S(1)} %pad_maximum_fusion.6), channel_id=1, source_target_pairs={{0,1},{1,2},{2,3},{4,5},{5,6},{6,7},{8,9},{9,10},{10,11},{12,13},{... | collective-permute-start | bytes 23048 | tf_op jit(solution)/shard_map/ppermute | solution.py:16
  47.4 1.3 collective-permute-start.6
  48.7 3.6 %collective-permute-start.2 = (f32[16,3,1,128]{3,0,2,1:T(8,128)S(1)}, f32[16,3,1,128]{3,0,2,1:T(8,128)S(1)}, u32[]{:S(2)}, u32[]{:S(2)}) collective-permute-start(f32[16,3,1,128]{3,0,2,1:T(8,128)S(1)} %pad_maximum_fusion), channel_id=1, source_target_pairs={{0,1},{1,2},{2,3},{4,5},{5,6},{6,7},{8,9},{9,10},{10,11},{12,13},{... | collective-permute-start | bytes 73736 | tf_op jit(solution)/shard_map/ppermute | solution.py:16
  55.0 0.5 fusion.72
  55.5 32.3 %all-reduce.1 = (f32[16]{0:T(128)S(1)}, f32[16]{0:T(128)S(1)}) all-reduce(f32[16]{0:T(128)S(1)} %get-tuple-element.114, f32[16]{0:T(128)S(1)} %get-tuple-element.129), channel_id=1, replica_groups=mesh['rep'=2,'cell'=4,'sub'=4] {'cell','sub'}, use_global_device_ids=true, to_apply=%region_4.5 | all-reduce | flops 32 | bytes 256 | tf_op jit(solution)/shard_map/psum | solution.py:67
  87.9 1.3 collective-permute-start.8
  89.2 1.3 collective-permute-start.9
  90.9 3.9 %collective-permute-done.9 = f32[16,1,1,128]{3,0,2,1:T(8,128)S(1)} collective-permute-done((f32[16,1,1,128]{3,0,2,1:T(8,128)S(1)}, f32[16,1,1,128]{3,0,2,1:T(8,128)S(1)}, u32[]{:S(2)}, u32[]{:S(2)}) %collective-permute-start.9) | collective-permute-done | bytes 8224 | tf_op jit(solution)/shard_map/ppermute | solution.py:17
  94.8 1.3 collective-permute-start.11
  96.1 3.0 %collective-permute-start.10 = (f32[16,3,1,128]{3,0,2,1:T(8,128)S(1)}, f32[16,3,1,128]{3,0,2,1:T(8,128)S(1)}, u32[]{:S(2)}, u32[]{:S(2)}) collective-permute-start(f32[16,3,1,128]{3,0,2,1:T(8,128)S(1)} %pad_maximum_fusion.1), channel_id=1, source_target_pairs={{0,1},{1,2},{2,3},{4,5},{5,6},{6,7},{8,9},{9,10},{10,11},{12,13},{... | collective-permute-start | bytes 73736 | tf_op jit(solution)/shard_map/ppermute | solution.py:16
  101.7 0.5 fusion.32
  102.2 29.8 %all-reduce = (f32[16]{0:T(128)S(1)}, f32[16]{0:T(128)S(1)}) all-reduce(f32[16]{0:T(128)S(1)} %get-tuple-element.78, f32[16]{0:T(128)S(1)} %fusion.32), channel_id=1, replica_groups=mesh['rep'=2,'cell'=4,'sub'=4] {'cell','sub'}, use_global_device_ids=true, to_apply=%region_9.10 | all-reduce | flops 32 | bytes 256 | tf_op jit(solution)/shard_map/psum | solution.py:67
  132.3 5.8 %all-reduce.2 = (f32[8]{0:T(128)S(1)}, f32[8]{0:T(128)S(1)}) all-reduce(f32[8]{0:T(128)S(1)} %get-tuple-element.49, f32[8]{0:T(128)S(1)} %get-tuple-element.48), channel_id=1, replica_groups=mesh['rep'=2,'cell'=4,'sub'=4] {'sub'}, use_global_device_ids=true, to_apply=%region_13.14 | all-reduce | flops 16 | bytes 128 | tf_op jit(solution)/shard_map/psum | solution.py:135
  138.0 8.4 %all-reduce.3 = (f32[8]{0:T(128)S(1)}, f32[8]{0:T(128)S(1)}) all-reduce(f32[8]{0:T(128)S(1)} %get-tuple-element.72, f32[8]{0:T(128)S(1)} %get-tuple-element.73), channel_id=1, replica_groups=mesh['rep'=2,'cell'=4,'sub'=4] {'cell'}, use_global_device_ids=true, to_apply=%region_14.15 | all-reduce | flops 16 | bytes 128 | tf_op jit(solution)/shard_map/psum | solution.py:134
  146.4 0.7 multiply_subtract_fusion
  (65 shorter events, 6.8 us)
Async XLA Ops:
  25.1 0.7 copy-start.1
  25.1 0.7 copy-start.2
  25.1 0.7 copy-start.3
  26.1 21.3 %collective-permute-start = (f32[16,1,1,128]{3,0,2,1:T(8,128)S(1)}, f32[16,1,1,128]{3,0,2,1:T(8,128)S(1)}, u32[]{:S(2)}, u32[]{:S(2)}) collective-permute-start(f32[16,1,1,128]{3,0,2,1:T(8,128)S(1)} %get-tuple-element.115), channel_id=1, source_target_pairs={{0,4},{4,8},{8,12},{1,5},{5,9},{9,13},{2,6},{6,10},{10,14},{3,7},{... | collective-permute-start | bytes 24584 | tf_op jit(solution)/shard_map/ppermute | solution.py:16
  31.0 16.4 %collective-permute-start.1 = (f32[16,1,1,128]{3,0,2,1:T(8,128)S(1)}, f32[16,1,1,128]{3,0,2,1:T(8,128)S(1)}, u32[]{:S(2)}, u32[]{:S(2)}) collective-permute-start(f32[16,1,1,128]{3,0,2,1:T(8,128)S(1)} %get-tuple-element.115), channel_id=1, source_target_pairs={{4,0},{8,4},{12,8},{5,1},{9,5},{13,9},{6,2},{10,6},{14,10},{7,3},{... | collective-permute-start | bytes 24584 | tf_op jit(solution)/shard_map/ppermute | solution.py:17
  32.3 0.7 copy-start
  33.0 6.2 %collective-permute-start.3 = (f32[5,1,1,128]{3,2,1,0:T(1,128)S(1)}, f32[5,1,1,128]{3,2,1,0:T(1,128)S(1)}, u32[]{:S(2)}, u32[]{:S(2)}) collective-permute-start(f32[5,1,1,128]{3,2,1,0:T(1,128)S(1)} %pad_maximum_fusion.7), channel_id=1, source_target_pairs={{0,4},{4,8},{8,12},{1,5},{5,9},{9,13},{2,6},{6,10},{10,14},{3,7},{... | collective-permute-start | bytes 7688 | tf_op jit(solution)/shard_map/ppermute | solution.py:16
  37.5 5.5 %collective-permute-start.4 = (f32[5,1,1,128]{3,2,1,0:T(1,128)S(1)}, f32[5,1,1,128]{3,2,1,0:T(1,128)S(1)}, u32[]{:S(2)}, u32[]{:S(2)}) collective-permute-start(f32[5,1,1,128]{3,2,1,0:T(1,128)S(1)} %pad_maximum_fusion.7), channel_id=1, source_target_pairs={{4,0},{8,4},{12,8},{5,1},{9,5},{13,9},{6,2},{10,6},{14,10},{7,3},{... | collective-permute-start | bytes 7688 | tf_op jit(solution)/shard_map/ppermute | solution.py:17
  43.0 10.0 %collective-permute-start.7 = (f32[5,3,1,128]{3,2,1,0:T(1,128)S(1)}, f32[5,3,1,128]{3,2,1,0:T(1,128)S(1)}, u32[]{:S(2)}, u32[]{:S(2)}) collective-permute-start(f32[5,3,1,128]{3,2,1,0:T(1,128)S(1)} %pad_maximum_fusion.6), channel_id=1, source_target_pairs={{1,0},{2,1},{3,2},{5,4},{6,5},{7,6},{9,8},{10,9},{11,10},{13,12},{... | collective-permute-start | bytes 23048 | tf_op jit(solution)/shard_map/ppermute | solution.py:17
  44.3 8.8 %collective-permute-start.5 = (f32[5,3,1,128]{3,2,1,0:T(1,128)S(1)}, f32[5,3,1,128]{3,2,1,0:T(1,128)S(1)}, u32[]{:S(2)}, u32[]{:S(2)}) collective-permute-start(f32[5,3,1,128]{3,2,1,0:T(1,128)S(1)} %pad_maximum_fusion.6), channel_id=1, source_target_pairs={{0,1},{1,2},{2,3},{4,5},{5,6},{6,7},{8,9},{9,10},{10,11},{12,13},{... | collective-permute-start | bytes 23048 | tf_op jit(solution)/shard_map/ppermute | solution.py:16
  47.4 6.5 %collective-permute-start.6 = (f32[16,3,1,128]{3,0,2,1:T(8,128)S(1)}, f32[16,3,1,128]{3,0,2,1:T(8,128)S(1)}, u32[]{:S(2)}, u32[]{:S(2)}) collective-permute-start(f32[16,3,1,128]{3,0,2,1:T(8,128)S(1)} %pad_maximum_fusion), channel_id=1, source_target_pairs={{1,0},{2,1},{3,2},{5,4},{6,5},{7,6},{9,8},{10,9},{11,10},{13,12},{... | collective-permute-start | bytes 73736 | tf_op jit(solution)/shard_map/ppermute | solution.py:17
  48.7 4.5 %collective-permute-start.2 = (f32[16,3,1,128]{3,0,2,1:T(8,128)S(1)}, f32[16,3,1,128]{3,0,2,1:T(8,128)S(1)}, u32[]{:S(2)}, u32[]{:S(2)}) collective-permute-start(f32[16,3,1,128]{3,0,2,1:T(8,128)S(1)} %pad_maximum_fusion), channel_id=1, source_target_pairs={{0,1},{1,2},{2,3},{4,5},{5,6},{6,7},{8,9},{9,10},{10,11},{12,13},{... | collective-permute-start | bytes 73736 | tf_op jit(solution)/shard_map/ppermute | solution.py:16
  87.9 2.9 %collective-permute-start.8 = (f32[16,1,1,128]{3,0,2,1:T(8,128)S(1)}, f32[16,1,1,128]{3,0,2,1:T(8,128)S(1)}, u32[]{:S(2)}, u32[]{:S(2)}) collective-permute-start(f32[16,1,1,128]{3,0,2,1:T(8,128)S(1)} %bitcast.216), channel_id=1, source_target_pairs={{0,4},{4,8},{8,12},{1,5},{5,9},{9,13},{2,6},{6,10},{10,14},{3,7},{... | collective-permute-start | bytes 24584 | tf_op jit(solution)/shard_map/ppermute | solution.py:16
  89.2 5.5 %collective-permute-start.9 = (f32[16,1,1,128]{3,0,2,1:T(8,128)S(1)}, f32[16,1,1,128]{3,0,2,1:T(8,128)S(1)}, u32[]{:S(2)}, u32[]{:S(2)}) collective-permute-start(f32[16,1,1,128]{3,0,2,1:T(8,128)S(1)} %bitcast.217), channel_id=1, source_target_pairs={{4,0},{8,4},{12,8},{5,1},{9,5},{13,9},{6,2},{10,6},{14,10},{7,3},{... | collective-permute-start | bytes 24584 | tf_op jit(solution)/shard_map/ppermute | solution.py:17
  94.8 5.8 %collective-permute-start.11 = (f32[16,3,1,128]{3,0,2,1:T(8,128)S(1)}, f32[16,3,1,128]{3,0,2,1:T(8,128)S(1)}, u32[]{:S(2)}, u32[]{:S(2)}) collective-permute-start(f32[16,3,1,128]{3,0,2,1:T(8,128)S(1)} %pad_maximum_fusion.1), channel_id=1, source_target_pairs={{1,0},{2,1},{3,2},{5,4},{6,5},{7,6},{9,8},{10,9},{11,10},{13,12},{... | collective-permute-start | bytes 73736 | tf_op jit(solution)/shard_map/ppermute | solution.py:17
  96.1 3.9 %collective-permute-start.10 = (f32[16,3,1,128]{3,0,2,1:T(8,128)S(1)}, f32[16,3,1,128]{3,0,2,1:T(8,128)S(1)}, u32[]{:S(2)}, u32[]{:S(2)}) collective-permute-start(f32[16,3,1,128]{3,0,2,1:T(8,128)S(1)} %pad_maximum_fusion.1), channel_id=1, source_target_pairs={{0,1},{1,2},{2,3},{4,5},{5,6},{6,7},{8,9},{9,10},{10,11},{12,13},{... | collective-permute-start | bytes 73736 | tf_op jit(solution)/shard_map/ppermute | solution.py:16
